TPU v7x, 32 devices: a whole 2x2x4 slice. The times are simulated.
32 devices in a mesh: leaf: 8 (over z, y), col: 4 (over x, core).
Axes of the slice: x: 2, y: 2, z: 4, core: 2. Of those that a mesh axis runs over, the one named last changes fastest.
Arguments:
- leaf_rhs: float32 [7168, 512], P('leaf', 'col'), may hold values from -6 to 6
- leaf_inverse: float32 [56, 128, 128], P('leaf'), may hold values from -0.5 to 0.5
- leaf_blocks: float32 [168, 128, 128], P('leaf'), may hold values from -0.1875 to 0.1875
- leaf_pattern: int32 [8, 21], P('leaf'), may hold values 0 or 1
- leaf_coupling: float32 [2048, 512], P('leaf'), may hold values from -0.0625 to 0.0625
- sep_rhs: float32 [1536, 512], P('leaf', 'col'), may hold values from -6 to 6
- sep_inverse: float32 [1536, 512], P('leaf', 'col'), may hold values from -0.25 to 0.25
- sep_coupling: float32 [1024, 512], P('leaf', 'col'), may hold values from -0.09375 to 0.09375
Outputs:
- leaf_solution: float32 [7168, 512], P('leaf', 'col')
- sep_solution: float32 [1536, 512], P('leaf', 'col')
Inputs may be any that keep to these rules, and one draw needn't show every extreme that they name: `leaf_pattern`: 1 where a factor block below the diagonal is nonzero, 0 where it is zero.
All inputs are finite; a program needn't handle non-finite values.
Results may differ from a plain program's by a relative error of at most 0.00011.
Values sent between devices are 32-bit elements; how exact they have to be, the bound alone decides.
A program may use at most 64 MiB of HBM per device.

v0:
```python
import functools

import jax
import jax.numpy as jnp
from jax import lax
from jax.experimental import pallas as pl
from jax.experimental.pallas import tpu as pltpu
from jax.sharding import PartitionSpec as P

HIGH = lax.Precision.HIGHEST
F32 = jnp.float32
BF16 = jnp.bfloat16
NN = ((1,), (0,))
NT = ((1,), (1,))


def from_partner(shard, axis, apart):
    return lax.ppermute(shard, axis, [(i, i ^ 1 << apart) for i in range(lax.axis_size(axis))])


def product(left_side, right_side):
    return jnp.dot(left_side, right_side, precision=HIGH, preferred_element_type=jnp.float32)


def product_first(left_side, right_side):
    return lax.dot_general(
        left_side,
        right_side,
        (((0,), (0,)), ((), ())),
        precision=HIGH,
        preferred_element_type=jnp.float32,
    )


def group_sizes(leaf_count):
    result = []
    for level_index in range(1, 5):
        group_span = 4**level_index
        if group_span // 4 < leaf_count:
            result.append(min(group_span, leaf_count))
    return result


def group_total(partial_value, group_size):
    bit_count = group_size.bit_length() - 1
    for bit_place in range(bit_count):
        partial_value = partial_value + from_partner(partial_value, "leaf", bit_place)
    return partial_value


def shards(
    leaf_rhs,
    leaf_inverse,
    leaf_blocks,
    leaf_pattern,
    leaf_coupling,
    sep_rhs,
    sep_inverse,
    sep_coupling,
):
    inverse_full, coupling_full = (
        lax.all_gather(sep_inverse, "col", axis=1, tiled=True),
        lax.all_gather(sep_coupling, "col", axis=1, tiled=True),
    )
    leaf_count = lax.axis_size("leaf")
    position = lax.axis_index("leaf")
    block_count = leaf_inverse.shape[0]
    block_rows = leaf_inverse.shape[1]
    columns = leaf_rhs.shape[1]
    sep_rows = inverse_full.shape[1]
    weighted = leaf_blocks * leaf_pattern[0].astype(jnp.float32)[:, None, None]
    rhs_blocks = leaf_rhs.reshape(block_count, block_rows, columns)
    column_starts = []
    running = 0
    for column_index in range(block_count):
        column_starts.append(running)
        running = running + block_count - 1 - column_index
    pending = [rhs_blocks[i] for i in range(block_count)]
    forward = []
    for column_index in range(block_count):
        solved = product(leaf_inverse[column_index], pending[column_index])
        forward.append(solved)
        below_count = block_count - 1 - column_index
        if below_count:
            pair_start = column_starts[column_index]
            column_blocks = weighted[pair_start : pair_start + below_count].reshape(
                below_count * block_rows, block_rows
            )
            update = product(column_blocks, solved).reshape(below_count, block_rows, columns)
            for later_index in range(below_count):
                pending[column_index + 1 + later_index] = (
                    pending[column_index + 1 + later_index] - update[later_index]
                )
    sizes_list = group_sizes(leaf_count)
    level_total = len(sizes_list)
    row_counts = [sep_rows // size_item for size_item in sizes_list]
    offsets = []
    running = 0
    for row_count in row_counts:
        offsets.append(running)
        running = running + row_count
    last_block = forward[-1]
    level_pieces = []
    for level_index in range(level_total):
        group_size = sizes_list[level_index]
        row_count = row_counts[level_index]
        row_offset = offsets[level_index]
        row_start = position % group_size * row_count
        coupling_rows = leaf_coupling[level_index * block_rows : (level_index + 1) * block_rows]
        partial_value = -product_first(coupling_rows, last_block)
        if level_index > 0:
            child_offset = offsets[level_index - 1]
            child_count = row_counts[level_index - 1]
            partial_value = partial_value - product_first(
                coupling_full[child_offset : child_offset + child_count], level_pieces[-1]
            )
        own_rows = (
            lax.dynamic_slice_in_dim(partial_value, row_start, row_count, 0)
            + sep_rhs[row_offset : row_offset + row_count]
        )
        partial_value = lax.dynamic_update_slice_in_dim(partial_value, own_rows, row_start, 0)
        summed = group_total(partial_value, group_size)
        level_pieces.append(product(inverse_full[row_offset : row_offset + row_count], summed))
    correction = jnp.zeros((block_rows, columns), jnp.float32)
    solution_pieces = [None] * level_total
    parent_full = None
    for level_index in reversed(range(level_total)):
        group_size = sizes_list[level_index]
        row_count = row_counts[level_index]
        row_offset = offsets[level_index]
        row_start = position % group_size * row_count
        target = level_pieces[level_index]
        if parent_full is not None:
            target = target - product(
                coupling_full[row_offset : row_offset + row_count], parent_full
            )
        partial_value = product_first(inverse_full[row_offset : row_offset + row_count], target)
        parent_full = group_total(partial_value, group_size)
        solution_pieces[level_index] = lax.dynamic_slice_in_dim(
            parent_full, row_start, row_count, 0
        )
        correction = correction + product(
            leaf_coupling[level_index * block_rows : (level_index + 1) * block_rows], parent_full
        )
    pending = list(forward)
    pending[-1] = pending[-1] - correction
    backward = [None] * block_count
    for column_index in reversed(range(block_count)):
        target = pending[column_index]
        below_count = block_count - 1 - column_index
        if below_count:
            pair_start = column_starts[column_index]
            column_blocks = weighted[pair_start : pair_start + below_count].reshape(
                below_count * block_rows, block_rows
            )
            later_blocks = jnp.concatenate(backward[column_index + 1 :], 0)
            target = target - product_first(column_blocks, later_blocks)
        backward[column_index] = product_first(leaf_inverse[column_index], target)
    return (jnp.concatenate(backward, 0), jnp.concatenate(solution_pieces, 0))


def halves(value):
    top = value.astype(BF16)
    return top, (value - top.astype(F32)).astype(BF16)


def mm(left_side, right_side, dims=NN):
    return lax.dot_general(
        left_side, right_side, (dims, ((), ())), preferred_element_type=F32
    )


def wide(left_top, left_low, right_both):
    n = right_both.shape[1] // 2
    both = mm(left_top, right_both)
    return both[:, :n] + both[:, n:] + mm(left_low, right_both[:, :n])


def tall(left_side, right_top, right_low, dims=NN):
    n = left_side.shape[0]
    top, low = halves(left_side)
    both = mm(jnp.concatenate([top, low], 0), right_top, dims)
    return both[:n] + both[n:] + mm(top, right_low, dims)


def whole_kernel(
    rhs_far, inv_far, blk_far, pat_far, cpl_far, srhs_far, sinv, scpl,
    out, sout,
    rhs, inv, blk, pat, cpl, srhs,
    l_top, l_low, xt_top, xt_low, solved, lifted,
    e_top, e_low, d1b, cb, d2b, d1_top, d1_low, c_top, c_low, d2_top, d2_low,
    pad, part, ra, acc, rb, tsend, trecv, xg, tmp, send, recv, near,
):
    leaf = lax.axis_index("leaf")
    col = lax.axis_index("col")
    y = lax.rem(leaf, 2)
    z0 = lax.rem(lax.div(leaf, 2), 2)
    z1 = lax.div(leaf, 4)
    core = lax.rem(col, 2)
    x = lax.div(col, 2)
    to_core = (leaf, col + 1 - 2 * core)
    to_x = (leaf, col + 2 - 4 * x)
    to_y = (leaf + 1 - 2 * y, col)
    to_z0 = (leaf + 2 - 4 * z0, col)
    to_z1 = (leaf + 4 - 8 * z1, col)

    barrier = pltpu.get_barrier_semaphore()
    partners = (to_core, to_x, to_y, to_z0, to_z1)
    for partner in partners:
        pl.semaphore_signal(
            barrier, inc=1, device_id=partner, device_id_type=pl.DeviceIdType.MESH
        )
    nb, br = inv.shape[0], inv.shape[1]
    n = rhs.shape[1]
    sep = cpl.shape[1]
    half = sep // 2
    r1, r2 = sep // 4, sep // 8
    w = n // 4
    starts = []
    running = 0
    for j in range(nb):
        starts.append(running)
        running += nb - 1 - j

    loads = []

    def fetch(src, dst):
        copy = pltpu.make_async_copy(src, dst, near.at[len(loads)])
        loads.append(copy)
        copy.start()
        return copy

    own = [
        fetch(sinv.at[pl.ds(0, r1)], d1b.at[z0, y, x, core]),
        fetch(scpl, cb.at[z0, y, x, core]),
        fetch(sinv.at[pl.ds(r1, r2)], d2b.at[z1, z0, y, x, core]),
    ]
    got_pat = fetch(pat_far, pat)
    got_inv = fetch(inv_far, inv)
    got_rhs = fetch(rhs_far, rhs)
    got_blk = []
    for j in range(nb - 1):
        box = pl.ds(starts[j], nb - 1 - j)
        got_blk.append(fetch(blk_far.at[box], blk.at[box]))
    got_cpl = fetch(cpl_far, cpl)
    got_srhs = fetch(srhs_far, srhs)


    copies = []

    def ship(src, dst, target):
        i = len(copies)
        copy = pltpu.make_async_remote_copy(
            src_ref=src, dst_ref=dst, send_sem=send.at[i], recv_sem=recv.at[i],
            device_id=target, device_id_type=pl.DeviceIdType.MESH,
        )
        copies.append(copy)
        copy.start()
        return copy

    got_pat.wait()
    got_inv.wait()
    got_rhs.wait()

    def at(i):
        return slice(i * br, (i + 1) * br)

    def load_column(j):
        if j < nb - 1:
            got_blk[j].wait()
        l_top[at(j), at(j)], l_low[at(j), at(j)] = halves(inv[j])
        for i in range(j + 1, nb):
            p = starts[j] + i - j - 1
            block = blk[p] * pat[0, p].astype(F32)
            l_top[at(i), at(j)], l_low[at(i), at(j)] = halves(block)

    pending = [rhs[at(i)] for i in range(nb)]
    forward = [None] * nb

    def forward_step(j):
        load_column(j)
        top, low = halves(pending[j])
        solved_j = wide(l_top[at(j), at(j)], l_low[at(j), at(j)], jnp.concatenate([top, low], 1))
        forward[j] = solved_j
        top, low = halves(solved_j)
        both = jnp.concatenate([top, low], 1)
        for i in range(j + 1, nb):
            pending[i] = pending[i] - wide(l_top[at(i), at(j)], l_low[at(i), at(j)], both)

    for j in range(nb):
        forward_step(j)
    got_cpl.wait()
    e_top[...], e_low[...] = halves(cpl[...])

    got_srhs.wait()
    last_t = forward[nb - 1].T

    def make_part(l):
        pad[...] = jnp.zeros_like(pad)
        if l == 0:
            pad[pl.ds(pl.multiple_of((2 * z0 + y) * r1, r1), r1), :] = srhs[0:r1]
        else:
            pad[pl.ds(pl.multiple_of(leaf * r2, r2), r2), :] = srhs[r1 : r1 + r2]
        term = pad[...].T - tall(last_t, e_top[at(l), :], e_low[at(l), :])
        for h in range(2):
            part[l, h] = term[:, h * half : (h + 1) * half].reshape(2, 2, w, half)

    def send_part(l):
        return (
            ship(part.at[l, 0, :, 1 - y], ra.at[l, 0], to_y),
            ship(part.at[l, 1, 1 - z0, :], ra.at[l, 1], to_z0),
        )

    make_part(0)
    make_part(1)
    for copy in own:
        copy.wait()
    pl.semaphore_wait(barrier, len(partners))

    orders = ("xyz", "yzx", "zxy")
    partner_of = {"x": to_x, "y": to_y, "z": to_z0}

    def row_parts(count):
        units = count // 8
        first = (units + 2) // 3
        second = (units - first + 1) // 2
        sizes = (first * 8, second * 8, count - 8 * (first + second))
        return ((0, sizes[0]), (sizes[0], sizes[1]), (sizes[0] + sizes[1], sizes[2]))

    def stage(ref, step, source=None, lead=()):
        sent = []
        for order, (begin, size) in zip(orders, row_parts(ref.shape[-2])):
            have = order[:step]
            where = lead + tuple(
                slice(None) if name in have else place
                for name, place in (("z", z0), ("y", y), ("x", x))
            ) + (core, pl.ds(begin, size))
            box = ref.at[where]
            src = box if source is None else source.at[pl.ds(begin, size)]
            sent.append(ship(src, box, partner_of[order[step]]))
        return sent

    def arrived(sent):
        for copy in sent:
            copy.wait_recv()

    every = (slice(None),)
    d1_a = stage(d1b, 0, sinv)
    a1 = send_part(0)
    c_a = stage(cb, 0, scpl)
    d2_z = ship(sinv.at[pl.ds(r1, r2)], d2b.at[z1, z0, y, x, core], to_z1)

    def second(l, pair):
        pair[0].wait_recv()
        acc[l, 0] = part[l, 0, :, y] + ra[l, 0]
        first = ship(acc.at[l, 0, 1 - z0], rb.at[l, 0], to_z0)
        pair[1].wait_recv()
        acc[l, 1] = part[l, 1, z0] + ra[l, 1]
        return first, ship(acc.at[l, 1, 1 - y], rb.at[l, 1], to_y)

    def total(l, pair):
        pair[0].wait_recv()
        pair[1].wait_recv()
        return jnp.concatenate([acc[l, 0, z0] + rb[l, 0], acc[l, 1, y] + rb[l, 1]], 1)

    row = lax.broadcasted_iota(jnp.int32, (br, br), 0)
    column = lax.broadcasted_iota(jnp.int32, (br, br), 1)
    unit = jnp.where(row == column, 1.0, 0.0).astype(F32)

    def backward_step(i):
        first = forward[i].T
        below = unit if i == nb - 1 else jnp.zeros((br, br), F32)
        target = jnp.concatenate([first, below], 0)
        if i < nb - 1:
            rest = slice((i + 1) * br, nb * br)
            target = target - (
                mm(xt_top[:, rest], l_top[rest, at(i)])
                + mm(xt_low[:, rest], l_top[rest, at(i)])
                + mm(xt_top[:, rest], l_low[rest, at(i)])
            )
        value = tall(target, l_top[at(i), at(i)], l_low[at(i), at(i)])
        xt_top[:, at(i)], xt_low[:, at(i)] = halves(value)
        solved[at(i), :] = value[:n].T
        top, low = halves(value[n:].T)
        lifted[at(i), 0:br] = top
        lifted[at(i), br : 2 * br] = low

    def spread(src, top_ref, low_ref, rows, lead):
        for k in range(lead):
            for c in range(4):
                if lead == 4:
                    tile = src[k // 2, k % 2, c // 2, c % 2]
                else:
                    tile = src[k // 4, k // 2 % 2, k % 2, c // 2, c % 2]
                where = (slice(k * rows, (k + 1) * rows), slice(c * tile.shape[1], (c + 1) * tile.shape[1]))
                top, low = halves(tile)
                top_ref[where] = top
                low_ref[where] = low

    arrived(d1_a)
    d1_b = stage(d1b, 1)
    b1 = second(0, a1)
    arrived(c_a)
    c_b = stage(cb, 1)
    arrived(d1_b)
    d1_c = stage(d1b, 2)
    a2 = send_part(1)
    arrived(c_b)
    c_c = stage(cb, 2)
    d2_z.wait_recv()
    d2_a = stage(d2b, 0, lead=every)
    s_1 = total(0, b1)
    b2 = second(1, a2)
    arrived(d1_c)
    d1_d = ship(d1b.at[:, :, :, core], d1b.at[:, :, :, core], to_core)
    backward_step(6)
    arrived(d2_a)
    d2_b = stage(d2b, 1, lead=every)
    d1_d.wait_recv()
    spread(d1b, d1_top, d1_low, r1, 4)
    z_1 = tall(s_1, d1_top[...], d1_low[...], NT)
    arrived(c_c)
    c_d = ship(cb.at[:, :, :, core], cb.at[:, :, :, core], to_core)
    s_2 = total(1, b2)
    c_d.wait_recv()
    spread(cb, c_top, c_low, r1, 4)
    tsend[...] = s_2 - tall(z_1, c_top[...], c_low[...])
    ts = ship(tsend, trecv, to_z1)
    arrived(d2_b)
    d2_c = stage(d2b, 2, lead=every)
    backward_step(5)
    backward_step(4)
    arrived(d2_c)
    d2_d = ship(d2b.at[:, :, :, :, core], d2b.at[:, :, :, :, core], to_core)
    backward_step(3)
    backward_step(2)
    d2_d.wait_recv()
    spread(d2b, d2_top, d2_low, r2, 8)
    ts.wait_recv()
    z_2 = tall(tsend[...] + trecv[...], d2_top[...], d2_low[...], NT)
    x_2 = tall(z_2, d2_top[...], d2_low[...])

    def give(l, value):
        xg[l, 0, z0, y] = value[:, :half]
        xg[l, 1, z0, y] = value[:, half:]
        return (
            ship(xg.at[l, 0, z0, y], xg.at[l, 0, z0, y], to_y),
            ship(xg.at[l, 1, z0, y], xg.at[l, 1, z0, y], to_z0),
        )

    def give_more(l, pair):
        pair[0].wait_recv()
        first = ship(xg.at[l, 0, z0], xg.at[l, 0, z0], to_z0)
        pair[1].wait_recv()
        return first, ship(xg.at[l, 1, :, y], xg.at[l, 1, :, y], to_y)

    def correction(l, pair):
        result = None
        for h in range(2):
            pair[h].wait_recv()
            top, low = halves(xg[l, h].reshape(n, half))
            lanes = slice(h * half, (h + 1) * half)
            e_t, e_l = e_top[at(l), lanes], e_low[at(l), lanes]
            term = mm(e_t, top, NT) + mm(e_t, low, NT) + mm(e_l, top, NT)
            result = term if result is None else result + term
        return result

    a2 = give(1, x_2)
    x_1 = tall(z_1 - tall(x_2, c_top[...], c_low[...], NT), d1_top[...], d1_low[...])
    a1 = give(0, x_1)
    a2 = give_more(1, a2)
    backward_step(1)
    a1 = give_more(0, a1)
    backward_step(0)
    fix = correction(1, a2)
    tmp[...] = xg[1, z1, :, :, :, pl.ds(pl.multiple_of(z0 * 2 * r2, 2 * r2), 2 * r2)].reshape(n, 2 * r2).T
    sout[r1 : r1 + r2, :] = tmp[pl.ds(pl.multiple_of(y * r2, r2), r2), :]
    fix = fix + correction(0, a1)
    top, low = halves(fix)
    both = jnp.concatenate([top, low], 1)
    for i in range(nb):
        out[at(i), :] = solved[at(i), :] - wide(lifted[at(i), 0:br], lifted[at(i), br : 2 * br], both)
    sout[0:r1, :] = xg[0, z0, :, :, :, pl.ds(pl.multiple_of(y * r1, r1), r1)].reshape(n, r1).T
    for copy in copies:
        copy.wait_send()


def fused(leaf_rhs, leaf_inverse, leaf_blocks, leaf_pattern, leaf_coupling, sep_rhs, sep_inverse, sep_coupling):
    rows, n = leaf_rhs.shape
    br = leaf_inverse.shape[1]
    sep = leaf_coupling.shape[1]
    half, w = sep // 2, n // 4
    r1, r2 = sep // 4, sep // 8
    tile = sep_inverse.shape[1]
    vm = pl.BlockSpec(memory_space=pltpu.VMEM)
    V = pltpu.VMEM
    return pl.pallas_call(
        whole_kernel,
        out_shape=(
            jax.ShapeDtypeStruct((rows, n), F32),
            jax.ShapeDtypeStruct(sep_rhs.shape, F32),
        ),
        in_specs=[pl.BlockSpec(memory_space=pl.ANY)] * 8,
        out_specs=(vm, vm),
        scratch_shapes=[
            V(leaf_rhs.shape, F32), V(leaf_inverse.shape, F32), V(leaf_blocks.shape, F32),
            pltpu.SMEM(leaf_pattern.shape, jnp.int32),
            V(leaf_coupling.shape, F32), V(sep_rhs.shape, F32),
            V((rows, rows), BF16), V((rows, rows), BF16),
            V((n + br, rows), BF16), V((n + br, rows), BF16),
            V((rows, n), F32), V((rows, 2 * br), BF16),
            V(leaf_coupling.shape, BF16), V(leaf_coupling.shape, BF16),
            V((2, 2, 2, 2, r1, tile), F32),
            V((2, 2, 2, 2, r1, tile), F32),
            V((2, 2, 2, 2, 2, r2, tile), F32),
            V((sep, sep), BF16), V((sep, sep), BF16),
            V((sep, sep), BF16), V((sep, sep), BF16),
            V((sep, sep), BF16), V((sep, sep), BF16),
            V((sep, n), F32),
            V((2, 2, 2, 2, w, half), F32),
            V((2, 2, 2, w, half), F32),
            V((2, 2, 2, w, half), F32),
            V((2, 2, w, half), F32),
            V((w, sep), F32), V((w, sep), F32),
            V((2, 2, 2, 2, w, half), F32),
            V((2 * r2, n), F32),
            pltpu.SemaphoreType.DMA((64,)),
            pltpu.SemaphoreType.DMA((64,)),
            pltpu.SemaphoreType.DMA((16,)),
        ],
        compiler_params=pltpu.CompilerParams(
            collective_id=0, has_side_effects=True, vmem_limit_bytes=62 * 1024 * 1024
        ),
    )(leaf_rhs, leaf_inverse, leaf_blocks, leaf_pattern, leaf_coupling, sep_rhs, sep_inverse, sep_coupling)


def pick(*args):
    leaf_rhs, leaf_inverse, _, _, leaf_coupling, _, sep_inverse, _ = args
    if (
        lax.axis_size("leaf") == 8
        and lax.axis_size("col") == 4
        and leaf_inverse.shape[1] == leaf_rhs.shape[1] == sep_inverse.shape[1]
        and leaf_coupling.shape[1] == 4 * sep_inverse.shape[1]
    ):
        return fused(*args)
    return shards(*args)


def solution(mesh):
    return jax.shard_map(
        pick,
        mesh=mesh,
        in_specs=(
            P("leaf", "col"),
            P("leaf", None, None),
            P("leaf", None, None),
            P("leaf", None),
            P("leaf", None),
            P("leaf", "col"),
            P("leaf", "col"),
            P("leaf", "col"),
        ),
        out_specs=(P("leaf", "col"), P("leaf", "col")),
        check_vma=False,
    )
```

profile of v0, /device:TPU:0, one launch (start us, length us, event | category | flops | bytes accessed | tf_op | source)
XLA Modules:
  0.0 46.3 jit_solution(18282287602654300057)
XLA Ops:
  0.6 42.3 %shard_map.95 = (f32[896,128]{1,0:T(8,128)}, f32[192,128]{1,0:T(8,128)}) custom-call(f32[896,128]{1,0:T(8,128)} %rhs_far.1, f32[7,128,128]{2,1,0:T(8,128)} %inv_far.1, f32[21,128,128]{2,1,0:T(8,128)} %blk_far.1, s32[1,21]{1,0:T(1,128)} %pat_far.1, f32[256,512]{1,0:T(8,128)} %cpl_far.1, f32[192,128]{1,0:T(8,128)} %srhs_far.1, f32[192,128]{1,0:T(8,128)} %sinv.1, ...), custom_call_target="tpu_custom_call" | custom-call | tf_op jit(solution)/shard_map/pallas_call | solution.py:497
  42.9 1.8 %copy.12 = f32[896,128]{1,0:T(8,128)} copy(f32[896,128]{1,0:T(8,128)} %get-tuple-element.4) | data formatting | bytes 917504
  44.7 1.5 %copy.13 = f32[192,128]{1,0:T(8,128)} copy(f32[192,128]{1,0:T(8,128)} %get-tuple-element.5) | data formatting | bytes 196608
where the time goes:
time: 46.5 us; the launch traced here: 46.3 us
  Pallas kernels  42.3 us (91%)
  local copies, waits for them, and re-layouts  3.35 us (7%)
  between operations  0.64 us (1%)
    pallas_call x1, Pallas kernels, fused(): pl.pallas_call(whole_kernel, out_shape=(jax.ShapeDtypeStruct((rows, n), F...  42.3 us
    unnamed x2, local copies, waits for them, and re-layouts  3.35 us

commit v1 on v0

--- a/solution.py
+++ b/solution.py
@@ -185,9 +185,9 @@
 
 def whole_kernel(
     rhs_far, inv_far, blk_far, pat_far, cpl_far, srhs_far, sinv, scpl,
-    out, sout,
+    solved, lifted, fixed, sout,
     rhs, inv, blk, pat, cpl, srhs,
-    l_top, l_low, xt_top, xt_low, solved, lifted,
+    l_top, l_low, xt_top, xt_low,
     e_top, e_low, d1b, cb, d2b, d1_top, d1_low, c_top, c_low, d2_top, d2_low,
     pad, part, ra, acc, rb, tsend, trecv, xg, tmp, send, recv, near,
 ):
@@ -477,9 +477,7 @@
     sout[r1 : r1 + r2, :] = tmp[pl.ds(pl.multiple_of(y * r2, r2), r2), :]
     fix = fix + correction(0, a1)
     top, low = halves(fix)
-    both = jnp.concatenate([top, low], 1)
-    for i in range(nb):
-        out[at(i), :] = solved[at(i), :] - wide(lifted[at(i), 0:br], lifted[at(i), br : 2 * br], both)
+    fixed[...] = jnp.concatenate([top, low], 1)
     sout[0:r1, :] = xg[0, z0, :, :, :, pl.ds(pl.multiple_of(y * r1, r1), r1)].reshape(n, r1).T
     for copy in copies:
         copy.wait_send()
@@ -494,21 +492,22 @@
     tile = sep_inverse.shape[1]
     vm = pl.BlockSpec(memory_space=pltpu.VMEM)
     V = pltpu.VMEM
-    return pl.pallas_call(
+    solved, lifted, fixed, sout = pl.pallas_call(
         whole_kernel,
         out_shape=(
-            jax.ShapeDtypeStruct((rows, n), F32),
-            jax.ShapeDtypeStruct(sep_rhs.shape, F32),
+            pltpu.VMEM((rows, n), F32),
+            pltpu.VMEM((rows, 2 * br), BF16),
+            pltpu.VMEM((br, 2 * n), BF16),
+            pltpu.VMEM(sep_rhs.shape, F32),
         ),
-        in_specs=[pl.BlockSpec(memory_space=pl.ANY)] * 8,
-        out_specs=(vm, vm),
+        in_specs=[pl.BlockSpec(memory_space=pltpu.HBM)] * 8,
+        out_specs=(vm, vm, vm, vm),
         scratch_shapes=[
             V(leaf_rhs.shape, F32), V(leaf_inverse.shape, F32), V(leaf_blocks.shape, F32),
             pltpu.SMEM(leaf_pattern.shape, jnp.int32),
             V(leaf_coupling.shape, F32), V(sep_rhs.shape, F32),
             V((rows, rows), BF16), V((rows, rows), BF16),
             V((n + br, rows), BF16), V((n + br, rows), BF16),
-            V((rows, n), F32), V((rows, 2 * br), BF16),
             V(leaf_coupling.shape, BF16), V(leaf_coupling.shape, BF16),
             V((2, 2, 2, 2, r1, tile), F32),
             V((2, 2, 2, 2, r1, tile), F32),
@@ -529,9 +528,36 @@
             pltpu.SemaphoreType.DMA((16,)),
         ],
         compiler_params=pltpu.CompilerParams(
-            collective_id=0, has_side_effects=True, vmem_limit_bytes=62 * 1024 * 1024
+            collective_id=0, has_side_effects=True, vmem_limit_bytes=65_800_000
         ),
     )(leaf_rhs, leaf_inverse, leaf_blocks, leaf_pattern, leaf_coupling, sep_rhs, sep_inverse, sep_coupling)
+
+    return pl.pallas_call(
+        finish_kernel,
+        out_shape=(
+            jax.ShapeDtypeStruct((rows, n), F32),
+            jax.ShapeDtypeStruct(sep_rhs.shape, F32),
+        ),
+        in_specs=[vm] * 4,
+        out_specs=[pl.BlockSpec(memory_space=pl.ANY)] * 2,
+        scratch_shapes=[V((rows, n), F32), pltpu.SemaphoreType.DMA((16,))],
+        compiler_params=pltpu.CompilerParams(vmem_limit_bytes=8 * 1024 * 1024),
+    )(solved, lifted, fixed, sout)
+
+
+def finish_kernel(solved, lifted, fixed, sout, out_far, sout_far, out, near):
+    br = fixed.shape[0]
+    copies = [pltpu.make_async_copy(sout, sout_far, near.at[0])]
+    copies[0].start()
+    both = fixed[...]
+    for i in range(solved.shape[0] // br):
+        rows = slice(i * br, (i + 1) * br)
+        out[rows, :] = solved[rows, :] - wide(lifted[rows, 0:br], lifted[rows, br : 2 * br], both)
+        copy = pltpu.make_async_copy(out.at[pl.ds(i * br, br)], out_far.at[pl.ds(i * br, br)], near.at[i + 1])
+        copy.start()
+        copies.append(copy)
+    for copy in copies:
+        copy.wait()
 
 
 def pick(*args):

time: 46.5 us -> 43 us (0.925)
  local copies, waits for them, and re-layouts: 3.35 us -> 0 us
    unnamed x2 -> x0, local copies, waits for them, and re-layouts: 3.35 us -> none
    pallas_call x1 -> x2, Pallas kernels: 42.3 us -> 42.2 us  [the longest x1 41.1 us: fused(): pl.pallas_call(whole_kernel, out_shape=(pltpu.VMEM((rows, n), F32), pltpu...]
where the time goes in v1:
time: 43 us; the launch traced here: 42.9 us
  Pallas kernels  42.2 us (98%)
  between operations  0.64 us (1%)
    pallas_call x1, Pallas kernels, fused(): pl.pallas_call(whole_kernel, out_shape=(pltpu.VMEM((rows, n), F32), pltpu...  41.1 us
    pallas_call x1, Pallas kernels, fused(): pl.pallas_call(finish_kernel, out_shape=(jax.ShapeDtypeStruct((rows, n),...  1.12 us

profile of v1, /device:TPU:0, one launch (start us, length us, event | category | flops | bytes accessed | tf_op | source)
XLA Modules:
  0.0 42.9 jit_solution(4439732868373528151)
XLA Ops:
  0.6 41.1 %shard_map.95 = (f32[896,128]{1,0:T(8,128)S(1)}, bf16[896,256]{1,0:T(8,128)(2,1)S(1)}, bf16[128,256]{1,0:T(8,128)(2,1)S(1)}, f32[192,128]{1,0:T(8,128)S(1)}) custom-call(f32[896,128]{1,0:T(8,128)} %rhs_far.1, f32[7,128,128]{2,1,0:T(8,128)} %inv_far.1, f32[21,128,128]{2,1,0:T(8,128)} %blk_far.1, s32[1,21]{1,0:T(1,128)} %pat_far.1, f32[256,512]{1,0:T(8,128)} %cpl_far.1, ...), custom_call_target="tpu_custom_call" | custom-call | tf_op jit(solution)/shard_map/pallas_call | solution.py:495
  41.8 1.1 %shard_map.96 = (f32[896,128]{1,0:T(8,128)}, f32[192,128]{1,0:T(8,128)}) custom-call(f32[896,128]{1,0:T(8,128)S(1)} %get-tuple-element.6.solved, bf16[896,256]{1,0:T(8,128)(2,1)S(1)} %get-tuple-element.7.lifted, bf16[128,256]{1,0:T(8,128)(2,1)S(1)} %get-tuple-element.8.fixed, f32[192,128]{1,0:T(8,128)S(1)} %get-tuple-element.9.sout), custom_call_target="tpu_custom_call" | custom-call | tf_op jit(solution)/shard_map/pallas_call | solution.py:535

commit v2 on v1

--- a/solution.py
+++ b/solution.py
@@ -183,13 +183,19 @@
     return both[:n] + both[n:] + mm(top, right_low, dims)
 
 
+def tall3(left_top, left_low, right_top, right_low, dims=NN):
+    n = left_top.shape[0]
+    both = mm(jnp.concatenate([left_top, left_low], 0), right_top, dims)
+    return both[:n] + both[n:] + mm(left_top, right_low, dims)
+
+
 def whole_kernel(
     rhs_far, inv_far, blk_far, pat_far, cpl_far, srhs_far, sinv, scpl,
     solved, lifted, fixed, sout,
     rhs, inv, blk, pat, cpl, srhs,
     l_top, l_low, xt_top, xt_low,
     e_top, e_low, d1b, cb, d2b, d1_top, d1_low, c_top, c_low, d2_top, d2_low,
-    pad, part, ra, acc, rb, tsend, trecv, xg, tmp, send, recv, near,
+    pad, part, ra, acc, rb, tsend, trecv, xg, tmp, u_top, u_low, v_top, v_low, gauge, send, recv, near,
 ):
     leaf = lax.axis_index("leaf")
     col = lax.axis_index("col")
@@ -222,60 +228,124 @@
         starts.append(running)
         running += nb - 1 - j
 
+    def rows_of(ref):
+        count = 1
+        for size in ref.shape:
+            count *= size
+        return count // 128
+
+    def land(semaphore, count):
+        box = gauge.at[pl.ds(0, count)]
+        pltpu.make_async_copy(box, box, semaphore).wait()
+
     loads = []
 
-    def fetch(src, dst):
-        copy = pltpu.make_async_copy(src, dst, near.at[len(loads)])
-        loads.append(copy)
-        copy.start()
-        return copy
-
-    own = [
-        fetch(sinv.at[pl.ds(0, r1)], d1b.at[z0, y, x, core]),
-        fetch(scpl, cb.at[z0, y, x, core]),
-        fetch(sinv.at[pl.ds(r1, r2)], d2b.at[z1, z0, y, x, core]),
-    ]
-    got_pat = fetch(pat_far, pat)
-    got_inv = fetch(inv_far, inv)
-    got_rhs = fetch(rhs_far, rhs)
+    def fetch(*pairs):
+        semaphore = near.at[len(loads)]
+        loads.append(semaphore)
+        count = 0
+        for src, dst in pairs:
+            pltpu.make_async_copy(src, dst, semaphore).start()
+            count += rows_of(dst)
+        return semaphore, count
+
+    pat_copy = pltpu.make_async_copy(pat_far, pat, near.at[0])
+    pat_copy.start()
+    loads.append(near.at[0])
+    got_main = fetch((inv_far, inv), (rhs_far, rhs))
     got_blk = []
     for j in range(nb - 1):
         box = pl.ds(starts[j], nb - 1 - j)
-        got_blk.append(fetch(blk_far.at[box], blk.at[box]))
-    got_cpl = fetch(cpl_far, cpl)
-    got_srhs = fetch(srhs_far, srhs)
-
-
-    copies = []
-
-    def ship(src, dst, target):
-        i = len(copies)
-        copy = pltpu.make_async_remote_copy(
-            src_ref=src, dst_ref=dst, send_sem=send.at[i], recv_sem=recv.at[i],
-            device_id=target, device_id_type=pl.DeviceIdType.MESH,
-        )
-        copies.append(copy)
-        copy.start()
-        return copy
-
-    got_pat.wait()
-    got_inv.wait()
-    got_rhs.wait()
+        got_blk.append(fetch((blk_far.at[box], blk.at[box])))
+    got_own = fetch(
+        (sinv.at[pl.ds(0, r1)], d1b.at[z0, y, x, core]),
+        (scpl, cb.at[z0, y, x, core]),
+        (sinv.at[pl.ds(r1, r2)], d2b.at[z1, z0, y, x, core]),
+    )
+    got_rest = fetch((cpl_far, cpl), (srhs_far, srhs))
+
+    shipped = []
+    groups = []
+
+    def ship(moves):
+        semaphore = recv.at[len(groups)]
+        groups.append(len(moves))
+        count = 0
+        for src, dst, target in moves:
+            pltpu.make_async_remote_copy(
+                src_ref=src, dst_ref=dst, send_sem=send.at[0], recv_sem=semaphore,
+                device_id=target, device_id_type=pl.DeviceIdType.MESH,
+            ).start()
+            count += rows_of(dst)
+        shipped.append(count)
+        return semaphore, count
+
+    def arrived(sent):
+        land(*sent)
+
+    partner_of = {"x": to_x, "y": to_y, "z": to_z0}
+    place_of = {"x": x, "y": y, "z": z0}
+    order_1 = (("xyz", 3), ("yzx", 3), ("zxy", 2))
+    order_c = (("yzx", 5), ("zyx", 5), ("xyz", 3), ("xzy", 3))
+    order_2 = (("xyz", 3), ("yzx", 3), ("zxy", 2))
+    every = (slice(None),)
+
+    def row_parts(count, orders):
+        units = count // 8
+        weight = sum(share for _, share in orders)
+        result = []
+        begin = seen = 0
+        for order, share in orders:
+            seen += share
+            end = seen * units // weight * 8
+            result.append((order, begin, end - begin))
+            begin = end
+        return result
+
+    def boxes(ref, orders, step, lead, fresh):
+        result = []
+        for order, begin, size in row_parts(ref.shape[-2], orders):
+            have = order[:step]
+            where = []
+            for name in "zyx":
+                if fresh and name == order[step - 1]:
+                    where.append(1 - place_of[name])
+                elif name in have:
+                    where.append(slice(None))
+                else:
+                    where.append(place_of[name])
+            result.append((order, ref.at[lead + tuple(where) + (core, pl.ds(begin, size))], begin, size))
+        return result
+
+    def stage(ref, orders, step, source=None, lead=()):
+        sent = []
+        for order, box, begin, size in boxes(ref, orders, step, lead, False):
+            src = box if source is None else source.at[pl.ds(begin, size)]
+            sent.append((src, box, partner_of[order[step]]))
+        return ship(sent)
+
+    def cross(ref, orders, step, lead=(), fresh=False):
+        return ship([(box, box, to_core) for _, box, _, _ in boxes(ref, orders, step, lead, fresh)])
 
     def at(i):
         return slice(i * br, (i + 1) * br)
 
     def load_column(j):
         if j < nb - 1:
-            got_blk[j].wait()
+            land(*got_blk[j])
         l_top[at(j), at(j)], l_low[at(j), at(j)] = halves(inv[j])
         for i in range(j + 1, nb):
             p = starts[j] + i - j - 1
             block = blk[p] * pat[0, p].astype(F32)
             l_top[at(i), at(j)], l_low[at(i), at(j)] = halves(block)
 
-    pending = [rhs[at(i)] for i in range(nb)]
+    pending = []
     forward = [None] * nb
+
+    def begin_forward():
+        pat_copy.wait()
+        land(*got_main)
+        pending.extend(rhs[at(i)] for i in range(nb))
 
     def forward_step(j):
         load_column(j)
@@ -287,13 +357,12 @@
         for i in range(j + 1, nb):
             pending[i] = pending[i] - wide(l_top[at(i), at(j)], l_low[at(i), at(j)], both)
 
-    for j in range(nb):
-        forward_step(j)
-    got_cpl.wait()
-    e_top[...], e_low[...] = halves(cpl[...])
-
-    got_srhs.wait()
-    last_t = forward[nb - 1].T
+    last_t = []
+
+    def end_forward():
+        land(*got_rest)
+        e_top[...], e_low[...] = halves(cpl[...])
+        last_t.append(forward[nb - 1].T)
 
     def make_part(l):
         pad[...] = jnp.zeros_like(pad)
@@ -301,66 +370,27 @@
             pad[pl.ds(pl.multiple_of((2 * z0 + y) * r1, r1), r1), :] = srhs[0:r1]
         else:
             pad[pl.ds(pl.multiple_of(leaf * r2, r2), r2), :] = srhs[r1 : r1 + r2]
-        term = pad[...].T - tall(last_t, e_top[at(l), :], e_low[at(l), :])
+        term = pad[...].T - tall(last_t[0], e_top[at(l), :], e_low[at(l), :])
         for h in range(2):
             part[l, h] = term[:, h * half : (h + 1) * half].reshape(2, 2, w, half)
 
     def send_part(l):
         return (
-            ship(part.at[l, 0, :, 1 - y], ra.at[l, 0], to_y),
-            ship(part.at[l, 1, 1 - z0, :], ra.at[l, 1], to_z0),
+            ship([(part.at[l, 0, :, 1 - y], ra.at[l, 0], to_y)]),
+            ship([(part.at[l, 1, 1 - z0, :], ra.at[l, 1], to_z0)]),
         )
 
-    make_part(0)
-    make_part(1)
-    for copy in own:
-        copy.wait()
-    pl.semaphore_wait(barrier, len(partners))
-
-    orders = ("xyz", "yzx", "zxy")
-    partner_of = {"x": to_x, "y": to_y, "z": to_z0}
-
-    def row_parts(count):
-        units = count // 8
-        first = (units + 2) // 3
-        second = (units - first + 1) // 2
-        sizes = (first * 8, second * 8, count - 8 * (first + second))
-        return ((0, sizes[0]), (sizes[0], sizes[1]), (sizes[0] + sizes[1], sizes[2]))
-
-    def stage(ref, step, source=None, lead=()):
-        sent = []
-        for order, (begin, size) in zip(orders, row_parts(ref.shape[-2])):
-            have = order[:step]
-            where = lead + tuple(
-                slice(None) if name in have else place
-                for name, place in (("z", z0), ("y", y), ("x", x))
-            ) + (core, pl.ds(begin, size))
-            box = ref.at[where]
-            src = box if source is None else source.at[pl.ds(begin, size)]
-            sent.append(ship(src, box, partner_of[order[step]]))
-        return sent
-
-    def arrived(sent):
-        for copy in sent:
-            copy.wait_recv()
-
-    every = (slice(None),)
-    d1_a = stage(d1b, 0, sinv)
-    a1 = send_part(0)
-    c_a = stage(cb, 0, scpl)
-    d2_z = ship(sinv.at[pl.ds(r1, r2)], d2b.at[z1, z0, y, x, core], to_z1)
-
     def second(l, pair):
-        pair[0].wait_recv()
+        arrived(pair[0])
         acc[l, 0] = part[l, 0, :, y] + ra[l, 0]
-        first = ship(acc.at[l, 0, 1 - z0], rb.at[l, 0], to_z0)
-        pair[1].wait_recv()
+        first = ship([(acc.at[l, 0, 1 - z0], rb.at[l, 0], to_z0)])
+        arrived(pair[1])
         acc[l, 1] = part[l, 1, z0] + ra[l, 1]
-        return first, ship(acc.at[l, 1, 1 - y], rb.at[l, 1], to_y)
+        return first, ship([(acc.at[l, 1, 1 - y], rb.at[l, 1], to_y)])
 
     def total(l, pair):
-        pair[0].wait_recv()
-        pair[1].wait_recv()
+        arrived(pair[0])
+        arrived(pair[1])
         return jnp.concatenate([acc[l, 0, z0] + rb[l, 0], acc[l, 1, y] + rb[l, 1]], 1)
 
     row = lax.broadcasted_iota(jnp.int32, (br, br), 0)
@@ -397,90 +427,124 @@
                 top_ref[where] = top
                 low_ref[where] = low
 
-    arrived(d1_a)
-    d1_b = stage(d1b, 1)
-    b1 = second(0, a1)
-    arrived(c_a)
-    c_b = stage(cb, 1)
-    arrived(d1_b)
-    d1_c = stage(d1b, 2)
-    a2 = send_part(1)
-    arrived(c_b)
-    c_c = stage(cb, 2)
-    d2_z.wait_recv()
-    d2_a = stage(d2b, 0, lead=every)
-    s_1 = total(0, b1)
-    b2 = second(1, a2)
-    arrived(d1_c)
-    d1_d = ship(d1b.at[:, :, :, core], d1b.at[:, :, :, core], to_core)
-    backward_step(6)
-    arrived(d2_a)
-    d2_b = stage(d2b, 1, lead=every)
-    d1_d.wait_recv()
-    spread(d1b, d1_top, d1_low, r1, 4)
-    z_1 = tall(s_1, d1_top[...], d1_low[...], NT)
-    arrived(c_c)
-    c_d = ship(cb.at[:, :, :, core], cb.at[:, :, :, core], to_core)
-    s_2 = total(1, b2)
-    c_d.wait_recv()
-    spread(cb, c_top, c_low, r1, 4)
-    tsend[...] = s_2 - tall(z_1, c_top[...], c_low[...])
-    ts = ship(tsend, trecv, to_z1)
-    arrived(d2_b)
-    d2_c = stage(d2b, 2, lead=every)
-    backward_step(5)
-    backward_step(4)
-    arrived(d2_c)
-    d2_d = ship(d2b.at[:, :, :, :, core], d2b.at[:, :, :, :, core], to_core)
-    backward_step(3)
-    backward_step(2)
-    d2_d.wait_recv()
-    spread(d2b, d2_top, d2_low, r2, 8)
-    ts.wait_recv()
-    z_2 = tall(tsend[...] + trecv[...], d2_top[...], d2_low[...], NT)
-    x_2 = tall(z_2, d2_top[...], d2_low[...])
-
     def give(l, value):
         xg[l, 0, z0, y] = value[:, :half]
         xg[l, 1, z0, y] = value[:, half:]
         return (
-            ship(xg.at[l, 0, z0, y], xg.at[l, 0, z0, y], to_y),
-            ship(xg.at[l, 1, z0, y], xg.at[l, 1, z0, y], to_z0),
+            ship([(xg.at[l, 0, z0, y], xg.at[l, 0, z0, y], to_y)]),
+            ship([(xg.at[l, 1, z0, y], xg.at[l, 1, z0, y], to_z0)]),
         )
 
     def give_more(l, pair):
-        pair[0].wait_recv()
-        first = ship(xg.at[l, 0, z0], xg.at[l, 0, z0], to_z0)
-        pair[1].wait_recv()
-        return first, ship(xg.at[l, 1, :, y], xg.at[l, 1, :, y], to_y)
-
-    def correction(l, pair):
-        result = None
-        for h in range(2):
-            pair[h].wait_recv()
-            top, low = halves(xg[l, h].reshape(n, half))
-            lanes = slice(h * half, (h + 1) * half)
-            e_t, e_l = e_top[at(l), lanes], e_low[at(l), lanes]
-            term = mm(e_t, top, NT) + mm(e_t, low, NT) + mm(e_l, top, NT)
-            result = term if result is None else result + term
-        return result
-
-    a2 = give(1, x_2)
-    x_1 = tall(z_1 - tall(x_2, c_top[...], c_low[...], NT), d1_top[...], d1_low[...])
-    a1 = give(0, x_1)
-    a2 = give_more(1, a2)
+        arrived(pair[0])
+        first = ship([(xg.at[l, 0, z0], xg.at[l, 0, z0], to_z0)])
+        arrived(pair[1])
+        return first, ship([(xg.at[l, 1, :, y], xg.at[l, 1, :, y], to_y)])
+
+    def against(top_ref, low_ref, l, h):
+        top, low = halves(xg[l, h].reshape(n, half))
+        lanes = slice(h * half, (h + 1) * half)
+        left = jnp.concatenate([top_ref[:, lanes], low_ref[:, lanes]], 0)
+        both = mm(left, top, NT)
+        return both[: 2 * br] + both[2 * br :] + mm(top_ref[:, lanes], low, NT)
+
+    def make_u():
+        tile = pl.ds(pl.multiple_of((2 * z0 + y) * r1, r1), r1)
+        u_top[0:br, :], u_low[0:br, :] = halves(tall3(e_top[at(0), :], e_low[at(0), :], d1_top[...], d1_low[...], NT))
+        u_top[br : 2 * br, :] = d1_top[:, tile].T
+        u_low[br : 2 * br, :] = d1_low[:, tile].T
+
+    def make_v():
+        value = tall3(u_top[...], u_low[...], c_top[...], c_low[...], NN)
+        v_top[0:br, :], v_low[0:br, :] = halves(cpl[at(1), :] - value[0:br])
+        v_top[br : 2 * br, :], v_low[br : 2 * br, :] = halves(-value[br : 2 * br])
+
+    begin_forward()
+    forward_step(0)
+    forward_step(1)
+    pl.semaphore_wait(barrier, len(partners))
+    d1_a = stage(d1b, order_1, 0, sinv)
+    c_a = stage(cb, order_c, 0, scpl)
+    d2_z = ship([(sinv.at[pl.ds(r1, r2)], d2b.at[z1, z0, y, x, core], to_z1)])
+    forward_step(2)
+    forward_step(3)
+    forward_step(4)
+    forward_step(5)
+    land(*got_own)
+    arrived(d1_a)
+    d1_b = stage(d1b, order_1, 1)
+    forward_step(6)
+    end_forward()
+    make_part(0)
+    a1 = send_part(0)
+    arrived(c_a)
+    c_b = stage(cb, order_c, 1)
+    make_part(1)
+    backward_step(6)
+    arrived(d1_b)
+    d1_c = stage(d1b, order_1, 2)
+    d1_d = cross(d1b, order_1, 2)
+    b1 = second(0, a1)
+    a2 = send_part(1)
+    arrived(c_b)
+    c_c = stage(cb, order_c, 2)
+    c_d = cross(cb, order_c, 2)
+    arrived(d2_z)
+    d2_a = stage(d2b, order_2, 0, lead=every)
+    backward_step(5)
+    backward_step(4)
+    arrived(d1_c)
+    d1_e = cross(d1b, order_1, 3, fresh=True)
+    b2 = second(1, a2)
+    backward_step(3)
+    arrived(d1_d)
+    arrived(d1_e)
+    spread(d1b, d1_top, d1_low, r1, 4)
+    s_1 = total(0, b1)
+    z_1 = tall(s_1, d1_top[...], d1_low[...], NT)
+    arrived(c_c)
+    c_e = cross(cb, order_c, 3, fresh=True)
+    arrived(d2_a)
+    d2_b = stage(d2b, order_2, 1, lead=every)
+    make_u()
+    arrived(c_d)
+    arrived(c_e)
+    spread(cb, c_top, c_low, r1, 4)
+    s_2 = total(1, b2)
+    tsend[...] = s_2 - tall(z_1, c_top[...], c_low[...])
+    ts = ship([(tsend, trecv, to_z1)])
+    g1 = give(0, z_1)
+    arrived(d2_b)
+    d2_c = stage(d2b, order_2, 2, lead=every)
+    d2_d = cross(d2b, order_2, 2, lead=every)
+    make_v()
+    g1 = give_more(0, g1)
+    backward_step(2)
     backward_step(1)
-    a1 = give_more(0, a1)
+    arrived(d2_c)
+    d2_e = cross(d2b, order_2, 3, lead=every, fresh=True)
     backward_step(0)
-    fix = correction(1, a2)
+    arrived(d2_d)
+    arrived(d2_e)
+    spread(d2b, d2_top, d2_low, r2, 8)
+    arrived(ts)
+    z_2 = tall(tsend[...] + trecv[...], d2_top[...], d2_low[...], NT)
+    x_2 = tall(z_2, d2_top[...], d2_low[...])
+    g2 = give(1, x_2)
+    arrived(g1[0])
+    arrived(g1[1])
+    base = against(u_top, u_low, 0, 0) + against(u_top, u_low, 0, 1)
+    g2 = give_more(1, g2)
+    arrived(g2[0])
+    base = base + against(v_top, v_low, 1, 0)
+    arrived(g2[1])
+    base = base + against(v_top, v_low, 1, 1)
+    top, low = halves(base[0:br])
+    fixed[...] = jnp.concatenate([top, low], 1)
+    sout[0:r1, :] = base[br : 2 * br]
     tmp[...] = xg[1, z1, :, :, :, pl.ds(pl.multiple_of(z0 * 2 * r2, 2 * r2), 2 * r2)].reshape(n, 2 * r2).T
     sout[r1 : r1 + r2, :] = tmp[pl.ds(pl.multiple_of(y * r2, r2), r2), :]
-    fix = fix + correction(0, a1)
-    top, low = halves(fix)
-    fixed[...] = jnp.concatenate([top, low], 1)
-    sout[0:r1, :] = xg[0, z0, :, :, :, pl.ds(pl.multiple_of(y * r1, r1), r1)].reshape(n, r1).T
-    for copy in copies:
-        copy.wait_send()
+    land(send.at[0], sum(shipped))
 
 
 def fused(leaf_rhs, leaf_inverse, leaf_blocks, leaf_pattern, leaf_coupling, sep_rhs, sep_inverse, sep_coupling):
@@ -523,9 +587,12 @@
             V((w, sep), F32), V((w, sep), F32),
             V((2, 2, 2, 2, w, half), F32),
             V((2 * r2, n), F32),
-            pltpu.SemaphoreType.DMA((64,)),
-            pltpu.SemaphoreType.DMA((64,)),
-            pltpu.SemaphoreType.DMA((16,)),
+            V((2 * br, sep), BF16), V((2 * br, sep), BF16),
+            V((2 * br, sep), BF16), V((2 * br, sep), BF16),
+            V((12 * 1024, 128), F32),
+            pltpu.SemaphoreType.DMA((1,)),
+            pltpu.SemaphoreType.DMA((34,)),
+            pltpu.SemaphoreType.DMA((10,)),
         ],
         compiler_params=pltpu.CompilerParams(
             collective_id=0, has_side_effects=True, vmem_limit_bytes=65_800_000
@@ -540,24 +607,22 @@
         ),
         in_specs=[vm] * 4,
         out_specs=[pl.BlockSpec(memory_space=pl.ANY)] * 2,
-        scratch_shapes=[V((rows, n), F32), pltpu.SemaphoreType.DMA((16,))],
+        scratch_shapes=[V((rows, n), F32), pltpu.SemaphoreType.DMA((2,))],
         compiler_params=pltpu.CompilerParams(vmem_limit_bytes=8 * 1024 * 1024),
     )(solved, lifted, fixed, sout)
 
 
 def finish_kernel(solved, lifted, fixed, sout, out_far, sout_far, out, near):
     br = fixed.shape[0]
-    copies = [pltpu.make_async_copy(sout, sout_far, near.at[0])]
-    copies[0].start()
+    sep_copy = pltpu.make_async_copy(sout, sout_far, near.at[0])
+    sep_copy.start()
     both = fixed[...]
     for i in range(solved.shape[0] // br):
         rows = slice(i * br, (i + 1) * br)
         out[rows, :] = solved[rows, :] - wide(lifted[rows, 0:br], lifted[rows, br : 2 * br], both)
-        copy = pltpu.make_async_copy(out.at[pl.ds(i * br, br)], out_far.at[pl.ds(i * br, br)], near.at[i + 1])
-        copy.start()
-        copies.append(copy)
-    for copy in copies:
-        copy.wait()
+        pltpu.make_async_copy(out.at[pl.ds(i * br, br)], out_far.at[pl.ds(i * br, br)], near.at[1]).start()
+    sep_copy.wait()
+    pltpu.make_async_copy(out, out_far, near.at[1]).wait()
 
 
 def pick(*args):

time: 43 us -> 39.5 us (0.919)
  Pallas kernels: 42.2 us -> 38.7 us
    pallas_call x1, Pallas kernels: 41.1 us -> 37.7 us  [fused(): pl.pallas_call(whole_kernel, out_shape=(pltpu.VMEM((rows, n), F32), pltpu...]
where the time goes in v2:
time: 39.5 us; the launch traced here: 39.4 us
  Pallas kernels  38.7 us (98%)
  between operations  0.64 us (2%)
    pallas_call x1, Pallas kernels, fused(): pl.pallas_call(whole_kernel, out_shape=(pltpu.VMEM((rows, n), F32), pltpu...  37.7 us
    pallas_call x1, Pallas kernels, fused(): pl.pallas_call(finish_kernel, out_shape=(jax.ShapeDtypeStruct((rows, n),...  0.99 us

profile of v2, /device:TPU:0, one launch (start us, length us, event | category | flops | bytes accessed | tf_op | source)
XLA Modules:
  0.0 39.4 jit_solution(12547564266996859108)
XLA Ops:
  0.6 37.7 %shard_map.95 = (f32[896,128]{1,0:T(8,128)S(1)}, bf16[896,256]{1,0:T(8,128)(2,1)S(1)}, bf16[128,256]{1,0:T(8,128)(2,1)S(1)}, f32[192,128]{1,0:T(8,128)S(1)}) custom-call(f32[896,128]{1,0:T(8,128)} %rhs_far.1, f32[7,128,128]{2,1,0:T(8,128)} %inv_far.1, f32[21,128,128]{2,1,0:T(8,128)} %blk_far.1, s32[1,21]{1,0:T(1,128)} %pat_far.1, f32[256,512]{1,0:T(8,128)} %cpl_far.1, ...), custom_call_target="tpu_custom_call" | custom-call | tf_op jit(solution)/shard_map/pallas_call | solution.py:559
  38.4 1.0 %shard_map.96 = (f32[896,128]{1,0:T(8,128)}, f32[192,128]{1,0:T(8,128)}) custom-call(f32[896,128]{1,0:T(8,128)S(1)} %get-tuple-element.6.solved, bf16[896,256]{1,0:T(8,128)(2,1)S(1)} %get-tuple-element.7.lifted, bf16[128,256]{1,0:T(8,128)(2,1)S(1)} %get-tuple-element.8.fixed, f32[192,128]{1,0:T(8,128)S(1)} %get-tuple-element.9.sout), custom_call_target="tpu_custom_call" | custom-call | tf_op jit(solution)/shard_map/pallas_call | solution.py:602

commit v3 on v2

--- a/solution.py
+++ b/solution.py
@@ -211,7 +211,8 @@
     to_z1 = (leaf + 4 - 8 * z1, col)
 
     barrier = pltpu.get_barrier_semaphore()
-    partners = (to_core, to_x, to_y, to_z0, to_z1)
+    to_yz = (leaf + 1 - 2 * y + 2 - 4 * z0, col)
+    partners = (to_core, to_x, to_y, to_z0, to_z1, to_yz)
     for partner in partners:
         pl.semaphore_signal(
             barrier, inc=1, device_id=partner, device_id_type=pl.DeviceIdType.MESH
@@ -254,8 +255,8 @@
     loads.append(near.at[0])
     got_main = fetch((inv_far, inv), (rhs_far, rhs))
     got_blk = []
-    for j in range(nb - 1):
-        box = pl.ds(starts[j], nb - 1 - j)
+    for begin, end in ((0, starts[1]), (starts[1], running)):
+        box = pl.ds(begin, end - begin)
         got_blk.append(fetch((blk_far.at[box], blk.at[box])))
     got_own = fetch(
         (sinv.at[pl.ds(0, r1)], d1b.at[z0, y, x, core]),
@@ -267,9 +268,7 @@
     shipped = []
     groups = []
 
-    def ship(moves):
-        semaphore = recv.at[len(groups)]
-        groups.append(len(moves))
+    def begin_moves(semaphore, moves):
         count = 0
         for src, dst, target in moves:
             pltpu.make_async_remote_copy(
@@ -278,16 +277,24 @@
             ).start()
             count += rows_of(dst)
         shipped.append(count)
-        return semaphore, count
+        return count
+
+    def ship(moves):
+        semaphore = recv.at[len(groups)]
+        groups.append(len(moves))
+        return semaphore, begin_moves(semaphore, moves)
+
+    def more(sent, moves):
+        return sent[0], sent[1] + begin_moves(sent[0], moves)
 
     def arrived(sent):
         land(*sent)
 
     partner_of = {"x": to_x, "y": to_y, "z": to_z0}
     place_of = {"x": x, "y": y, "z": z0}
-    order_1 = (("xyz", 3), ("yzx", 3), ("zxy", 2))
+    order_1 = (("yzx", 3), ("zyx", 3), ("xyz", 1), ("xzy", 1))
     order_c = (("yzx", 5), ("zyx", 5), ("xyz", 3), ("xzy", 3))
-    order_2 = (("xyz", 3), ("yzx", 3), ("zxy", 2))
+    order_2 = (("yzx", 5), ("zyx", 5), ("xyz", 3), ("xzy", 3))
     every = (slice(None),)
 
     def row_parts(count, orders):
@@ -302,36 +309,59 @@
             begin = end
         return result
 
-    def boxes(ref, orders, step, lead, fresh):
-        result = []
+    def tile(ref, lead, begin, size, far):
+        where = tuple(1 - place_of[name] if name in far else place_of[name] for name in "zyx")
+        return ref.at[lead + where + (core, pl.ds(begin, size))]
+
+    def first_wave(ref, orders, lead=()):
+        near_moves, last_moves = [], []
+        parts = row_parts(ref.shape[-2], orders)
+        for k in range(3):
+            for order, begin, size in parts:
+                box = tile(ref, lead, begin, size, "")
+                move = (box, box, partner_of[order[k]])
+                (last_moves if k == 2 else near_moves).append(move)
+        started = ship(near_moves)
+        last = ship(last_moves)
+        return started, last
+
+    def second_wave(ref, orders, sent, lead=()):
+        near_moves, last_moves = [], []
         for order, begin, size in row_parts(ref.shape[-2], orders):
-            have = order[:step]
+            p, q, r = order
+            box = tile(ref, lead, begin, size, p)
+            near_moves.append((box, box, partner_of[q]))
+            last_moves.append((box, box, partner_of[r]))
+            box = tile(ref, lead, begin, size, q)
+            last_moves.append((box, box, partner_of[r]))
+        started = ship(near_moves)
+        return started, more(sent[1], last_moves)
+
+    def third_wave(ref, orders, sent, lead=()):
+        moves = []
+        for order, begin, size in row_parts(ref.shape[-2], orders):
+            box = tile(ref, lead, begin, size, order[:2])
+            moves.append((box, box, partner_of[order[2]]))
+        return more(sent[1], moves)
+
+    def cross(ref, orders, fresh, lead=()):
+        moves = []
+        for order, begin, size in row_parts(ref.shape[-2], orders):
             where = []
             for name in "zyx":
-                if fresh and name == order[step - 1]:
-                    where.append(1 - place_of[name])
-                elif name in have:
+                if name != order[2]:
                     where.append(slice(None))
                 else:
-                    where.append(place_of[name])
-            result.append((order, ref.at[lead + tuple(where) + (core, pl.ds(begin, size))], begin, size))
-        return result
-
-    def stage(ref, orders, step, source=None, lead=()):
-        sent = []
-        for order, box, begin, size in boxes(ref, orders, step, lead, False):
-            src = box if source is None else source.at[pl.ds(begin, size)]
-            sent.append((src, box, partner_of[order[step]]))
-        return ship(sent)
-
-    def cross(ref, orders, step, lead=(), fresh=False):
-        return ship([(box, box, to_core) for _, box, _, _ in boxes(ref, orders, step, lead, fresh)])
+                    where.append(1 - place_of[name] if fresh else place_of[name])
+            box = ref.at[lead + tuple(where) + (core, pl.ds(begin, size))]
+            moves.append((box, box, to_core))
+        return ship(moves)
 
     def at(i):
         return slice(i * br, (i + 1) * br)
 
     def load_column(j):
-        if j < nb - 1:
+        if j < 2:
             land(*got_blk[j])
         l_top[at(j), at(j)], l_low[at(j), at(j)] = halves(inv[j])
         for i in range(j + 1, nb):
@@ -375,23 +405,25 @@
             part[l, h] = term[:, h * half : (h + 1) * half].reshape(2, 2, w, half)
 
     def send_part(l):
-        return (
-            ship([(part.at[l, 0, :, 1 - y], ra.at[l, 0], to_y)]),
-            ship([(part.at[l, 1, 1 - z0, :], ra.at[l, 1], to_z0)]),
-        )
-
-    def second(l, pair):
-        arrived(pair[0])
-        acc[l, 0] = part[l, 0, :, y] + ra[l, 0]
-        first = ship([(acc.at[l, 0, 1 - z0], rb.at[l, 0], to_z0)])
-        arrived(pair[1])
-        acc[l, 1] = part[l, 1, z0] + ra[l, 1]
-        return first, ship([(acc.at[l, 1, 1 - y], rb.at[l, 1], to_y)])
-
-    def total(l, pair):
-        arrived(pair[0])
-        arrived(pair[1])
-        return jnp.concatenate([acc[l, 0, z0] + rb[l, 0], acc[l, 1, y] + rb[l, 1]], 1)
+        first = ship([(part.at[l, 0, 1 - z0, 1 - y], ra.at[l, 0, 0], to_y)])
+        other = ship([(part.at[l, 1, 1 - z0, 1 - y], ra.at[l, 1, 0], to_z0)])
+        last = ship([
+            (part.at[l, 0, z0, 1 - y], ra.at[l, 0, 1], to_y),
+            (part.at[l, 1, 1 - z0, y], ra.at[l, 1, 1], to_z0),
+        ])
+        return first, other, last
+
+    def second(l, sent):
+        arrived(sent[0])
+        acc[l, 0] = part[l, 0, 1 - z0, y] + ra[l, 0, 0]
+        last = more(sent[2], [(acc.at[l, 0], rb.at[l, 0], to_z0)])
+        arrived(sent[1])
+        acc[l, 1] = part[l, 1, z0, 1 - y] + ra[l, 1, 0]
+        return more(last, [(acc.at[l, 1], rb.at[l, 1], to_y)])
+
+    def total(l, sent):
+        arrived(sent)
+        return jnp.concatenate([part[l, h, z0, y] + ra[l, h, 1] + rb[l, h] for h in range(2)], 1)
 
     row = lax.broadcasted_iota(jnp.int32, (br, br), 0)
     column = lax.broadcasted_iota(jnp.int32, (br, br), 1)
@@ -427,26 +459,40 @@
                 top_ref[where] = top
                 low_ref[where] = low
 
-    def give(l, value):
+    def place(l, value):
         xg[l, 0, z0, y] = value[:, :half]
         xg[l, 1, z0, y] = value[:, half:]
-        return (
-            ship([(xg.at[l, 0, z0, y], xg.at[l, 0, z0, y], to_y)]),
-            ship([(xg.at[l, 1, z0, y], xg.at[l, 1, z0, y], to_z0)]),
-        )
-
-    def give_more(l, pair):
-        arrived(pair[0])
-        first = ship([(xg.at[l, 0, z0], xg.at[l, 0, z0], to_z0)])
-        arrived(pair[1])
-        return first, ship([(xg.at[l, 1, :, y], xg.at[l, 1, :, y], to_y)])
-
-    def against(top_ref, low_ref, l, h):
-        top, low = halves(xg[l, h].reshape(n, half))
-        lanes = slice(h * half, (h + 1) * half)
-        left = jnp.concatenate([top_ref[:, lanes], low_ref[:, lanes]], 0)
-        both = mm(left, top, NT)
-        return both[: 2 * br] + both[2 * br :] + mm(top_ref[:, lanes], low, NT)
+
+    def give(l, value):
+        place(l, value)
+        box, other_box = xg.at[l, 0, z0, y], xg.at[l, 1, z0, y]
+        first = ship([(box, box, to_y)])
+        other = ship([(other_box, other_box, to_z0)])
+        return first, other, ship([(box, box, to_z0), (other_box, other_box, to_y)])
+
+    def give_more(l, sent):
+        arrived(sent[0])
+        box = xg.at[l, 0, z0, 1 - y]
+        last = more(sent[2], [(box, box, to_z0)])
+        arrived(sent[1])
+        box = xg.at[l, 1, 1 - z0, y]
+        return more(last, [(box, box, to_y)])
+
+    def give_all(l, value):
+        place(l, value)
+        box = xg.at[l, :, z0, y]
+        return ship([(box, box, target) for target in (to_yz, to_y, to_z0)])
+
+    def against(top_ref, low_ref, l):
+        result = None
+        for h in range(2):
+            top, low = halves(xg[l, h].reshape(n, half))
+            lanes = slice(h * half, (h + 1) * half)
+            left = jnp.concatenate([top_ref[:, lanes], low_ref[:, lanes]], 0)
+            both = mm(left, top, NT)
+            term = both[: 2 * br] + both[2 * br :] + mm(top_ref[:, lanes], low, NT)
+            result = term if result is None else result + term
+        return result
 
     def make_u():
         tile = pl.ds(pl.multiple_of((2 * z0 + y) * r1, r1), r1)
@@ -460,85 +506,81 @@
         v_top[br : 2 * br, :], v_low[br : 2 * br, :] = halves(-value[br : 2 * br])
 
     begin_forward()
+    land(*got_own)
+    pl.semaphore_wait(barrier, len(partners))
+    d1_s = first_wave(d1b, order_1)
+    c_s = first_wave(cb, order_c)
     forward_step(0)
     forward_step(1)
-    pl.semaphore_wait(barrier, len(partners))
-    d1_a = stage(d1b, order_1, 0, sinv)
-    c_a = stage(cb, order_c, 0, scpl)
-    d2_z = ship([(sinv.at[pl.ds(r1, r2)], d2b.at[z1, z0, y, x, core], to_z1)])
     forward_step(2)
     forward_step(3)
     forward_step(4)
     forward_step(5)
-    land(*got_own)
-    arrived(d1_a)
-    d1_b = stage(d1b, order_1, 1)
+    d2_z = ship([(sinv.at[pl.ds(r1, r2)], d2b.at[z1, z0, y, x, core], to_z1)])
+    arrived(d1_s[0])
+    d1_s = second_wave(d1b, order_1, d1_s)
     forward_step(6)
     end_forward()
+    arrived(c_s[0])
+    c_s = second_wave(cb, order_c, c_s)
     make_part(0)
     a1 = send_part(0)
-    arrived(c_a)
-    c_b = stage(cb, order_c, 1)
     make_part(1)
+    arrived(d1_s[0])
+    d1_l = third_wave(d1b, order_1, d1_s)
+    d1_d = cross(d1b, order_1, False)
+    b1 = second(0, a1)
     backward_step(6)
-    arrived(d1_b)
-    d1_c = stage(d1b, order_1, 2)
-    d1_d = cross(d1b, order_1, 2)
-    b1 = second(0, a1)
+    arrived(d2_z)
+    d2_s = first_wave(d2b, order_2, lead=every)
     a2 = send_part(1)
-    arrived(c_b)
-    c_c = stage(cb, order_c, 2)
-    c_d = cross(cb, order_c, 2)
-    arrived(d2_z)
-    d2_a = stage(d2b, order_2, 0, lead=every)
     backward_step(5)
+    arrived(c_s[0])
+    c_l = third_wave(cb, order_c, c_s)
+    c_d = cross(cb, order_c, False)
     backward_step(4)
-    arrived(d1_c)
-    d1_e = cross(d1b, order_1, 3, fresh=True)
-    b2 = second(1, a2)
-    backward_step(3)
+    arrived(d1_l)
+    d1_e = cross(d1b, order_1, True)
+    arrived(d2_s[0])
+    d2_s = second_wave(d2b, order_2, d2_s, lead=every)
     arrived(d1_d)
     arrived(d1_e)
     spread(d1b, d1_top, d1_low, r1, 4)
+    b2 = second(1, a2)
     s_1 = total(0, b1)
     z_1 = tall(s_1, d1_top[...], d1_low[...], NT)
-    arrived(c_c)
-    c_e = cross(cb, order_c, 3, fresh=True)
-    arrived(d2_a)
-    d2_b = stage(d2b, order_2, 1, lead=every)
-    make_u()
+    arrived(c_l)
+    c_e = cross(cb, order_c, True)
     arrived(c_d)
     arrived(c_e)
     spread(cb, c_top, c_low, r1, 4)
+    make_u()
+    g1 = give(0, z_1)
+    arrived(d2_s[0])
+    d2_l = third_wave(d2b, order_2, d2_s, lead=every)
     s_2 = total(1, b2)
     tsend[...] = s_2 - tall(z_1, c_top[...], c_low[...])
     ts = ship([(tsend, trecv, to_z1)])
-    g1 = give(0, z_1)
-    arrived(d2_b)
-    d2_c = stage(d2b, order_2, 2, lead=every)
-    d2_d = cross(d2b, order_2, 2, lead=every)
+    backward_step(3)
     make_v()
+    d2_d = cross(d2b, order_2, False, lead=every)
     g1 = give_more(0, g1)
     backward_step(2)
     backward_step(1)
-    arrived(d2_c)
-    d2_e = cross(d2b, order_2, 3, lead=every, fresh=True)
-    backward_step(0)
+    arrived(d2_l)
+    d2_e = cross(d2b, order_2, True, lead=every)
     arrived(d2_d)
     arrived(d2_e)
     spread(d2b, d2_top, d2_low, r2, 8)
     arrived(ts)
     z_2 = tall(tsend[...] + trecv[...], d2_top[...], d2_low[...], NT)
     x_2 = tall(z_2, d2_top[...], d2_low[...])
-    g2 = give(1, x_2)
-    arrived(g1[0])
-    arrived(g1[1])
-    base = against(u_top, u_low, 0, 0) + against(u_top, u_low, 0, 1)
-    g2 = give_more(1, g2)
-    arrived(g2[0])
-    base = base + against(v_top, v_low, 1, 0)
-    arrived(g2[1])
-    base = base + against(v_top, v_low, 1, 1)
+    g2 = give_all(1, x_2)
+    arrived(g1)
+    base = against(u_top, u_low, 0)
+    backward_step(0)
+    arrived(g2)
+    base = base + against(v_top, v_low, 1)
     top, low = halves(base[0:br])
     fixed[...] = jnp.concatenate([top, low], 1)
     sout[0:r1, :] = base[br : 2 * br]
@@ -582,7 +624,7 @@
             V((sep, n), F32),
             V((2, 2, 2, 2, w, half), F32),
             V((2, 2, 2, w, half), F32),
-            V((2, 2, 2, w, half), F32),
+            V((2, 2, w, half), F32),
             V((2, 2, w, half), F32),
             V((w, sep), F32), V((w, sep), F32),
             V((2, 2, 2, 2, w, half), F32),
@@ -591,8 +633,8 @@
             V((2 * br, sep), BF16), V((2 * br, sep), BF16),
             V((12 * 1024, 128), F32),
             pltpu.SemaphoreType.DMA((1,)),
-            pltpu.SemaphoreType.DMA((34,)),
-            pltpu.SemaphoreType.DMA((10,)),
+            pltpu.SemaphoreType.DMA((27,)),
+            pltpu.SemaphoreType.DMA((6,)),
         ],
         compiler_params=pltpu.CompilerParams(
             collective_id=0, has_side_effects=True, vmem_limit_bytes=65_800_000

time: 39.5 us -> 34 us (0.86)
  Pallas kernels: 38.7 us -> 33.2 us
    pallas_call x1, Pallas kernels: 37.7 us -> 32.2 us  [fused(): pl.pallas_call(whole_kernel, out_shape=(pltpu.VMEM((rows, n), F32), pltpu...]
where the time goes in v3:
time: 34 us; the launch traced here: 33.9 us
  Pallas kernels  33.2 us (98%)
  between operations  0.64 us (2%)
    pallas_call x1, Pallas kernels, fused(): pl.pallas_call(whole_kernel, out_shape=(pltpu.VMEM((rows, n), F32), pltpu...  32.2 us
    pallas_call x1, Pallas kernels, fused(): pl.pallas_call(finish_kernel, out_shape=(jax.ShapeDtypeStruct((rows, n),...  0.99 us

profile of v3, /device:TPU:0, one launch (start us, length us, event | category | flops | bytes accessed | tf_op | source)
XLA Modules:
  0.0 33.9 jit_solution(2429767947722649696)
XLA Ops:
  0.6 32.2 %shard_map.95 = (f32[896,128]{1,0:T(8,128)S(1)}, bf16[896,256]{1,0:T(8,128)(2,1)S(1)}, bf16[128,256]{1,0:T(8,128)(2,1)S(1)}, f32[192,128]{1,0:T(8,128)S(1)}) custom-call(f32[896,128]{1,0:T(8,128)} %rhs_far.1, f32[7,128,128]{2,1,0:T(8,128)} %inv_far.1, f32[21,128,128]{2,1,0:T(8,128)} %blk_far.1, s32[1,21]{1,0:T(1,128)} %pat_far.1, f32[256,512]{1,0:T(8,128)} %cpl_far.1, ...), custom_call_target="tpu_custom_call" | custom-call | tf_op jit(solution)/shard_map/pallas_call | solution.py:601
  32.9 1.0 %shard_map.96 = (f32[896,128]{1,0:T(8,128)}, f32[192,128]{1,0:T(8,128)}) custom-call(f32[896,128]{1,0:T(8,128)S(1)} %get-tuple-element.6.solved, bf16[896,256]{1,0:T(8,128)(2,1)S(1)} %get-tuple-element.7.lifted, bf16[128,256]{1,0:T(8,128)(2,1)S(1)} %get-tuple-element.8.fixed, f32[192,128]{1,0:T(8,128)S(1)} %get-tuple-element.9.sout), custom_call_target="tpu_custom_call" | custom-call | tf_op jit(solution)/shard_map/pallas_call | solution.py:644

commit v4 on v3

--- a/solution.py
+++ b/solution.py
@@ -195,7 +195,7 @@
     rhs, inv, blk, pat, cpl, srhs,
     l_top, l_low, xt_top, xt_low,
     e_top, e_low, d1b, cb, d2b, d1_top, d1_low, c_top, c_low, d2_top, d2_low,
-    pad, part, ra, acc, rb, tsend, trecv, xg, tmp, u_top, u_low, v_top, v_low, gauge, send, recv, near,
+    pad, part, ra, acc, rb, tsend, trecv, xg, tmp, u_top, u_low, v_top, v_low, q_top, q_low, r_top, r_low, gauge, send, recv, near,
 ):
     leaf = lax.axis_index("leaf")
     col = lax.axis_index("col")
@@ -205,14 +205,21 @@
     core = lax.rem(col, 2)
     x = lax.div(col, 2)
     to_core = (leaf, col + 1 - 2 * core)
-    to_x = (leaf, col + 2 - 4 * x)
-    to_y = (leaf + 1 - 2 * y, col)
-    to_z0 = (leaf + 2 - 4 * z0, col)
     to_z1 = (leaf + 4 - 8 * z1, col)
 
+    def across(names):
+        target_leaf, target_col = leaf, col
+        if "y" in names:
+            target_leaf = target_leaf + 1 - 2 * y
+        if "z" in names:
+            target_leaf = target_leaf + 2 - 4 * z0
+        if "x" in names:
+            target_col = target_col + 2 - 4 * x
+        return target_leaf, target_col
+
+    to_y, to_z0, to_yz = across("y"), across("z"), across("yz")
     barrier = pltpu.get_barrier_semaphore()
-    to_yz = (leaf + 1 - 2 * y + 2 - 4 * z0, col)
-    partners = (to_core, to_x, to_y, to_z0, to_z1, to_yz)
+    partners = (to_core, to_z1) + tuple(across(names) for names in ('x', 'y', 'yz', 'z'))
     for partner in partners:
         pl.semaphore_signal(
             barrier, inc=1, device_id=partner, device_id_type=pl.DeviceIdType.MESH
@@ -253,16 +260,16 @@
     pat_copy = pltpu.make_async_copy(pat_far, pat, near.at[0])
     pat_copy.start()
     loads.append(near.at[0])
+    got_own = fetch(
+        (sinv.at[pl.ds(0, r1)], d1b.at[z0, y, x, core]),
+        (scpl, cb.at[z0, y, x, core]),
+        (sinv.at[pl.ds(r1, r2)], d2b.at[z1, z0, y, x, core]),
+    )
     got_main = fetch((inv_far, inv), (rhs_far, rhs))
     got_blk = []
     for begin, end in ((0, starts[1]), (starts[1], running)):
         box = pl.ds(begin, end - begin)
         got_blk.append(fetch((blk_far.at[box], blk.at[box])))
-    got_own = fetch(
-        (sinv.at[pl.ds(0, r1)], d1b.at[z0, y, x, core]),
-        (scpl, cb.at[z0, y, x, core]),
-        (sinv.at[pl.ds(r1, r2)], d2b.at[z1, z0, y, x, core]),
-    )
     got_rest = fetch((cpl_far, cpl), (srhs_far, srhs))
 
     shipped = []
@@ -290,7 +297,7 @@
     def arrived(sent):
         land(*sent)
 
-    partner_of = {"x": to_x, "y": to_y, "z": to_z0}
+    partner_of = {name: across(name) for name in "xyz"}
     place_of = {"x": x, "y": y, "z": z0}
     order_1 = (("yzx", 3), ("zyx", 3), ("xyz", 1), ("xzy", 1))
     order_c = (("yzx", 5), ("zyx", 5), ("xyz", 3), ("xzy", 3))
@@ -325,15 +332,19 @@
         last = ship(last_moves)
         return started, last
 
-    def second_wave(ref, orders, sent, lead=()):
+    def second_wave(ref, orders, sent, short, lead=()):
         near_moves, last_moves = [], []
         for order, begin, size in row_parts(ref.shape[-2], orders):
             p, q, r = order
             box = tile(ref, lead, begin, size, p)
+            if short:
+                near_moves.append((box, box, across(q + r)))
             near_moves.append((box, box, partner_of[q]))
             last_moves.append((box, box, partner_of[r]))
             box = tile(ref, lead, begin, size, q)
             last_moves.append((box, box, partner_of[r]))
+        if short:
+            return None, more(sent[1], near_moves + last_moves)
         started = ship(near_moves)
         return started, more(sent[1], last_moves)
 
@@ -404,7 +415,13 @@
         for h in range(2):
             part[l, h] = term[:, h * half : (h + 1) * half].reshape(2, 2, w, half)
 
-    def send_part(l):
+    def send_part(l, short):
+        if short:
+            return ship([
+                (part.at[l, :, 1 - z0, 1 - y], ra.at[l, 0], to_yz),
+                (part.at[l, :, z0, 1 - y], ra.at[l, 1], to_y),
+                (part.at[l, :, 1 - z0, y], ra.at[l, 2], to_z0),
+            ])
         first = ship([(part.at[l, 0, 1 - z0, 1 - y], ra.at[l, 0, 0], to_y)])
         other = ship([(part.at[l, 1, 1 - z0, 1 - y], ra.at[l, 1, 0], to_z0)])
         last = ship([
@@ -421,8 +438,12 @@
         acc[l, 1] = part[l, 1, z0, 1 - y] + ra[l, 1, 0]
         return more(last, [(acc.at[l, 1], rb.at[l, 1], to_y)])
 
-    def total(l, sent):
+    def total(l, sent, short):
         arrived(sent)
+        if short:
+            return jnp.concatenate(
+                [part[l, h, z0, y] + ra[l, 0, h] + (ra[l, 1, h] + ra[l, 2, h]) for h in range(2)], 1
+            )
         return jnp.concatenate([part[l, h, z0, y] + ra[l, h, 1] + rb[l, h] for h in range(2)], 1)
 
     row = lax.broadcasted_iota(jnp.int32, (br, br), 0)
@@ -488,9 +509,8 @@
         for h in range(2):
             top, low = halves(xg[l, h].reshape(n, half))
             lanes = slice(h * half, (h + 1) * half)
-            left = jnp.concatenate([top_ref[:, lanes], low_ref[:, lanes]], 0)
-            both = mm(left, top, NT)
-            term = both[: 2 * br] + both[2 * br :] + mm(top_ref[:, lanes], low, NT)
+            both = mm(top_ref[:, lanes], jnp.concatenate([top, low], 0), NT)
+            term = both[:, :n] + both[:, n:] + mm(low_ref[:, lanes], top, NT)
             result = term if result is None else result + term
         return result
 
@@ -505,86 +525,111 @@
         v_top[0:br, :], v_low[0:br, :] = halves(cpl[at(1), :] - value[0:br])
         v_top[br : 2 * br, :], v_low[br : 2 * br, :] = halves(-value[br : 2 * br])
 
+    def make_q():
+        pair = pl.ds(pl.multiple_of((2 * z1 + z0) * 2 * r2, 2 * r2), 2 * r2)
+        q_top[0 : 2 * br, :], q_low[0 : 2 * br, :] = halves(
+            tall3(v_top[...], v_low[...], d2_top[...], d2_low[...], NT)
+        )
+        q_top[2 * br :, :] = d2_top[:, pair].T
+        q_low[2 * br :, :] = d2_low[:, pair].T
+
+    def make_r():
+        r_top[...], r_low[...] = halves(tall3(q_top[...], q_low[...], d2_top[...], d2_low[...], NN))
+
+    def rows_part(c):
+        return pl.ds(c * (w // 2), w // 2)
+
+    def give_part(l, c, sent):
+        rows = rows_part(c)
+        value = tsend[rows, :] + trecv[rows, :]
+        xg[l, 0, z0, y, rows] = value[:, :half]
+        xg[l, 1, z0, y, rows] = value[:, half:]
+        box = xg.at[l, :, z0, y, rows]
+        moves = [(box, box, target) for target in (to_yz, to_y, to_z0)]
+        return ship(moves) if sent is None else more(sent, moves)
+
     begin_forward()
     land(*got_own)
     pl.semaphore_wait(barrier, len(partners))
     d1_s = first_wave(d1b, order_1)
-    c_s = first_wave(cb, order_c)
     forward_step(0)
     forward_step(1)
+    c_s = first_wave(cb, order_c)
     forward_step(2)
     forward_step(3)
     forward_step(4)
-    forward_step(5)
     d2_z = ship([(sinv.at[pl.ds(r1, r2)], d2b.at[z1, z0, y, x, core], to_z1)])
     arrived(d1_s[0])
-    d1_s = second_wave(d1b, order_1, d1_s)
+    d1_s = second_wave(d1b, order_1, d1_s, False)
+    forward_step(5)
     forward_step(6)
     end_forward()
     arrived(c_s[0])
-    c_s = second_wave(cb, order_c, c_s)
+    c_s = second_wave(cb, order_c, c_s, False)
     make_part(0)
-    a1 = send_part(0)
+    a1 = send_part(0, False)
     make_part(1)
+    a2 = send_part(1, False)
     arrived(d1_s[0])
     d1_l = third_wave(d1b, order_1, d1_s)
+    b1 = second(0, a1)
+    arrived(c_s[0])
+    c_l = third_wave(cb, order_c, c_s)
+    backward_step(6)
     d1_d = cross(d1b, order_1, False)
-    b1 = second(0, a1)
-    backward_step(6)
     arrived(d2_z)
     d2_s = first_wave(d2b, order_2, lead=every)
-    a2 = send_part(1)
     backward_step(5)
-    arrived(c_s[0])
-    c_l = third_wave(cb, order_c, c_s)
     c_d = cross(cb, order_c, False)
     backward_step(4)
     arrived(d1_l)
     d1_e = cross(d1b, order_1, True)
-    arrived(d2_s[0])
-    d2_s = second_wave(d2b, order_2, d2_s, lead=every)
     arrived(d1_d)
     arrived(d1_e)
     spread(d1b, d1_top, d1_low, r1, 4)
     b2 = second(1, a2)
-    s_1 = total(0, b1)
-    z_1 = tall(s_1, d1_top[...], d1_low[...], NT)
     arrived(c_l)
     c_e = cross(cb, order_c, True)
+    arrived(d2_s[0])
+    d2_s = second_wave(d2b, order_2, d2_s, False, lead=every)
+    s_1 = total(0, b1, False)
+    z_1 = tall(s_1, d1_top[...], d1_low[...], NT)
     arrived(c_d)
     arrived(c_e)
     spread(cb, c_top, c_low, r1, 4)
     make_u()
     g1 = give(0, z_1)
+    s_2 = total(1, b2, False)
+    tsend[...] = s_2 - tall(z_1, c_top[...], c_low[...])
+    ts = [ship([(tsend.at[rows_part(c)], trecv.at[rows_part(c)], to_z1)]) for c in range(2)]
     arrived(d2_s[0])
     d2_l = third_wave(d2b, order_2, d2_s, lead=every)
-    s_2 = total(1, b2)
-    tsend[...] = s_2 - tall(z_1, c_top[...], c_low[...])
-    ts = ship([(tsend, trecv, to_z1)])
     backward_step(3)
     make_v()
+    g1 = give_more(0, g1)
     d2_d = cross(d2b, order_2, False, lead=every)
-    g1 = give_more(0, g1)
     backward_step(2)
     backward_step(1)
+    arrived(ts[0])
+    g2 = give_part(1, 0, None)
     arrived(d2_l)
     d2_e = cross(d2b, order_2, True, lead=every)
+    arrived(ts[1])
+    g2 = give_part(1, 1, g2)
     arrived(d2_d)
     arrived(d2_e)
     spread(d2b, d2_top, d2_low, r2, 8)
-    arrived(ts)
-    z_2 = tall(tsend[...] + trecv[...], d2_top[...], d2_low[...], NT)
-    x_2 = tall(z_2, d2_top[...], d2_low[...])
-    g2 = give_all(1, x_2)
+    make_q()
+    make_r()
     arrived(g1)
     base = against(u_top, u_low, 0)
     backward_step(0)
     arrived(g2)
-    base = base + against(v_top, v_low, 1)
-    top, low = halves(base[0:br])
+    rest = against(r_top, r_low, 1)
+    top, low = halves(base[0:br] + rest[0:br])
     fixed[...] = jnp.concatenate([top, low], 1)
-    sout[0:r1, :] = base[br : 2 * br]
-    tmp[...] = xg[1, z1, :, :, :, pl.ds(pl.multiple_of(z0 * 2 * r2, 2 * r2), 2 * r2)].reshape(n, 2 * r2).T
+    sout[0:r1, :] = base[br : 2 * br] + rest[br : 2 * br]
+    tmp[...] = rest[2 * br :]
     sout[r1 : r1 + r2, :] = tmp[pl.ds(pl.multiple_of(y * r2, r2), r2), :]
     land(send.at[0], sum(shipped))
 
@@ -623,7 +668,7 @@
             V((sep, sep), BF16), V((sep, sep), BF16),
             V((sep, n), F32),
             V((2, 2, 2, 2, w, half), F32),
-            V((2, 2, 2, w, half), F32),
+            V((2, 3, 2, w, half), F32),
             V((2, 2, w, half), F32),
             V((2, 2, w, half), F32),
             V((w, sep), F32), V((w, sep), F32),
@@ -631,9 +676,11 @@
             V((2 * r2, n), F32),
             V((2 * br, sep), BF16), V((2 * br, sep), BF16),
             V((2 * br, sep), BF16), V((2 * br, sep), BF16),
+            V((2 * br + 2 * r2, sep), BF16), V((2 * br + 2 * r2, sep), BF16),
+            V((2 * br + 2 * r2, sep), BF16), V((2 * br + 2 * r2, sep), BF16),
             V((12 * 1024, 128), F32),
             pltpu.SemaphoreType.DMA((1,)),
-            pltpu.SemaphoreType.DMA((27,)),
+            pltpu.SemaphoreType.DMA((28,)),
             pltpu.SemaphoreType.DMA((6,)),
         ],
         compiler_params=pltpu.CompilerParams(

time: 34 us -> 31.7 us (0.932)
  Pallas kernels: 33.2 us -> 30.9 us
    pallas_call x1, Pallas kernels: 32.2 us -> 29.9 us  [fused(): pl.pallas_call(whole_kernel, out_shape=(pltpu.VMEM((rows, n), F32), pltpu...]
where the time goes in v4:
time: 31.7 us; the launch traced here: 31.6 us
  Pallas kernels  30.9 us (97%)
  between operations  0.64 us (2%)
    pallas_call x1, Pallas kernels, fused(): pl.pallas_call(whole_kernel, out_shape=(pltpu.VMEM((rows, n), F32), pltpu...  29.9 us
    pallas_call x1, Pallas kernels, fused(): pl.pallas_call(finish_kernel, out_shape=(jax.ShapeDtypeStruct((rows, n),...  0.99 us

profile of v4, /device:TPU:0, one launch (start us, length us, event | category | flops | bytes accessed | tf_op | source)
XLA Modules:
  0.0 31.6 jit_solution(17591268213748583495)
XLA Ops:
  0.6 29.9 %shard_map.95 = (f32[896,128]{1,0:T(8,128)S(1)}, bf16[896,256]{1,0:T(8,128)(2,1)S(1)}, bf16[128,256]{1,0:T(8,128)(2,1)S(1)}, f32[192,128]{1,0:T(8,128)S(1)}) custom-call(f32[896,128]{1,0:T(8,128)} %rhs_far.1, f32[7,128,128]{2,1,0:T(8,128)} %inv_far.1, f32[21,128,128]{2,1,0:T(8,128)} %blk_far.1, s32[1,21]{1,0:T(1,128)} %pat_far.1, f32[256,512]{1,0:T(8,128)} %cpl_far.1, ...), custom_call_target="tpu_custom_call" | custom-call | tf_op jit(solution)/shard_map/pallas_call | solution.py:646
  30.6 1.0 %shard_map.96 = (f32[896,128]{1,0:T(8,128)}, f32[192,128]{1,0:T(8,128)}) custom-call(f32[896,128]{1,0:T(8,128)S(1)} %get-tuple-element.6.solved, bf16[896,256]{1,0:T(8,128)(2,1)S(1)} %get-tuple-element.7.lifted, bf16[128,256]{1,0:T(8,128)(2,1)S(1)} %get-tuple-element.8.fixed, f32[192,128]{1,0:T(8,128)S(1)} %get-tuple-element.9.sout), custom_call_target="tpu_custom_call" | custom-call | tf_op jit(solution)/shard_map/pallas_call | solution.py:691

commit v5 on v4

--- a/solution.py
+++ b/solution.py
@@ -594,10 +594,10 @@
     d2_s = second_wave(d2b, order_2, d2_s, False, lead=every)
     s_1 = total(0, b1, False)
     z_1 = tall(s_1, d1_top[...], d1_low[...], NT)
+    make_u()
     arrived(c_d)
     arrived(c_e)
     spread(cb, c_top, c_low, r1, 4)
-    make_u()
     g1 = give(0, z_1)
     s_2 = total(1, b2, False)
     tsend[...] = s_2 - tall(z_1, c_top[...], c_low[...])
@@ -616,6 +616,7 @@
     d2_e = cross(d2b, order_2, True, lead=every)
     arrived(ts[1])
     g2 = give_part(1, 1, g2)
+    backward_step(0)
     arrived(d2_d)
     arrived(d2_e)
     spread(d2b, d2_top, d2_low, r2, 8)
@@ -623,7 +624,6 @@
     make_r()
     arrived(g1)
     base = against(u_top, u_low, 0)
-    backward_step(0)
     arrived(g2)
     rest = against(r_top, r_low, 1)
     top, low = halves(base[0:br] + rest[0:br])

time: 31.7 us -> 31.6 us (level)
  no operation moved by 1% of the time
where the time goes in v5:
time: 31.6 us; the launch traced here: 31.5 us
  Pallas kernels  30.8 us (97%)
  between operations  0.64 us (2%)
    pallas_call x1, Pallas kernels, fused(): pl.pallas_call(whole_kernel, out_shape=(pltpu.VMEM((rows, n), F32), pltpu...  29.8 us
    pallas_call x1, Pallas kernels, fused(): pl.pallas_call(finish_kernel, out_shape=(jax.ShapeDtypeStruct((rows, n),...  1 us

profile of v5, /device:TPU:0, one launch (start us, length us, event | category | flops | bytes accessed | tf_op | source)
XLA Modules:
  0.0 31.5 jit_solution(3761542156885180995)
XLA Ops:
  0.6 29.8 %shard_map.95 = (f32[896,128]{1,0:T(8,128)S(1)}, bf16[896,256]{1,0:T(8,128)(2,1)S(1)}, bf16[128,256]{1,0:T(8,128)(2,1)S(1)}, f32[192,128]{1,0:T(8,128)S(1)}) custom-call(f32[896,128]{1,0:T(8,128)} %rhs_far.1, f32[7,128,128]{2,1,0:T(8,128)} %inv_far.1, f32[21,128,128]{2,1,0:T(8,128)} %blk_far.1, s32[1,21]{1,0:T(1,128)} %pat_far.1, f32[256,512]{1,0:T(8,128)} %cpl_far.1, ...), custom_call_target="tpu_custom_call" | custom-call | tf_op jit(solution)/shard_map/pallas_call | solution.py:646
  30.5 1.0 %shard_map.96 = (f32[896,128]{1,0:T(8,128)}, f32[192,128]{1,0:T(8,128)}) custom-call(f32[896,128]{1,0:T(8,128)S(1)} %get-tuple-element.6.solved, bf16[896,256]{1,0:T(8,128)(2,1)S(1)} %get-tuple-element.7.lifted, bf16[128,256]{1,0:T(8,128)(2,1)S(1)} %get-tuple-element.8.fixed, f32[192,128]{1,0:T(8,128)S(1)} %get-tuple-element.9.sout), custom_call_target="tpu_custom_call" | custom-call | tf_op jit(solution)/shard_map/pallas_call | solution.py:691
